TPU v7x, 256 devices: a whole 4x4x8 slice. The times are simulated.
256 devices in a mesh: rep: 32 (over x, y, core), tp: 8 (over z).
Axes of the slice: x: 4, y: 4, z: 8, core: 2. Of those that a mesh axis runs over, the one named last changes fastest.
Arguments:
- hidden_in: bfloat16 [3072, 8192], P('rep', 'tp'), may hold values from -6 to 6
- queries: bfloat16 [3072, 8192], P('rep', 'tp'), may hold values from -20 to 20
- cache_keys: bfloat16 [3072, 128, 1024], P('rep', None, 'tp'), may hold values from -6 to 6
- cached_value_rows: bfloat16 [3072, 128, 1024], P('rep', None, 'tp'), may hold values from -6 to 6
- cache_lengths: int32 [3072], P('rep'), may hold values from 1 to 128, 98304 in all
- base_key_matrix: bfloat16 [8192, 1024], P(None, 'tp'), may hold values from -0.0625 to 0.0625
- base_value_matrix: bfloat16 [8192, 1024], P(None, 'tp'), may hold values from -0.0625 to 0.0625
- shrink_weights: bfloat16 [128, 8192, 128], P('rep', 'tp'), may hold values from -0.0625 to 0.0625
- pooled_up_weights: bfloat16 [128, 2, 64, 1024], P('rep', None, None, 'tp'), may hold values from -0.75 to 0.75
- block_owner: int32 [768, 1], P('rep'), may hold values from 0 to 31; in each aligned block of 24 rows (0 to 23, 24 to 47, ...) at most 2 rows name the same one
- block_slot: int32 [768], P('rep'), may hold values from 0 to 3
Outputs:
- new_keys: bfloat16 [3072, 1024], P('rep', 'tp')
- new_values: bfloat16 [3072, 1024], P('rep', 'tp')
- context: bfloat16 [3072, 8192], P('rep', 'tp')
Inputs may be any that keep to these rules, and one draw needn't show every extreme that they name: `block_owner`: among the 24 blocks of one replica group at most 2 name the same owner, and some group in every draw has 2 blocks with one owner.
All inputs are finite; a program needn't handle non-finite values. No bound on the sum of `cache_lengths` on one device may be relied on, other than what follows from the above.
Results may differ from a plain program's by a relative error of at most 0.0055.
Values may be sent and summed in bfloat16 or wider, within the bound.
A program may use at most 128 MiB of HBM per device.

v0:
```python
import jax
import jax.numpy as jnp
from jax import lax
from jax.sharding import PartitionSpec as P

HEAD_SIZE = 128
BLK = 4
adapter_scale = 0.5
masked_score = -1e30


def attend(group_queries, key_cache, value_cache, lengths, fresh_keys, fresh_values):
    rows_here = group_queries.shape[0]
    head_groups = key_cache.shape[2] // HEAD_SIZE
    group_size = group_queries.shape[1] // (head_groups * HEAD_SIZE)
    window = key_cache.shape[1]
    inverse_root = HEAD_SIZE ** (-0.5)
    query_heads = group_queries.reshape(rows_here, head_groups, group_size, HEAD_SIZE)
    key_heads = key_cache.reshape(rows_here, window, head_groups, HEAD_SIZE)
    value_heads = value_cache.reshape(rows_here, window, head_groups, HEAD_SIZE)
    scores = (
        jnp.einsum("rkgd,rtkd->rkgt", query_heads, key_heads, preferred_element_type=jnp.float32)
        * inverse_root
    )
    own_score = (
        jnp.einsum(
            "rkgd,rkd->rkg",
            query_heads,
            fresh_keys.reshape(rows_here, head_groups, HEAD_SIZE),
            preferred_element_type=jnp.float32,
        )
        * inverse_root
    )
    visible = (jnp.arange(window, dtype=jnp.int32)[None, :] < lengths[:, None])[:, None, None, :]
    highest = jnp.maximum(jnp.max(jnp.where(visible, scores, masked_score), axis=-1), own_score)
    exp_terms = jnp.where(visible, jnp.exp(scores - highest[..., None]), 0.0)
    own_term = jnp.exp(own_score - highest)
    denominator = jnp.sum(exp_terms, axis=-1) + own_term
    weights = (exp_terms / denominator[..., None]).astype(jnp.bfloat16)
    own_weight = (own_term / denominator).astype(jnp.bfloat16)
    context = jnp.einsum(
        "rkgt,rtkd->rkgd", weights, value_heads, preferred_element_type=jnp.float32
    )
    context = context + own_weight.astype(jnp.float32)[..., None] * fresh_values.reshape(
        rows_here, head_groups, 1, HEAD_SIZE
    ).astype(jnp.float32)
    return context.reshape(rows_here, -1).astype(jnp.bfloat16)


def earlier_ranks(owners):
    span_count = owners.shape[-1]
    matching = owners[..., :, None] == owners[..., None, :]
    before = jnp.arange(span_count)[:, None] > jnp.arange(span_count)[None, :]
    return jnp.sum((matching & before).astype(jnp.int32), axis=-1)


def slot_layout(owners_all, slots_all, myself, replicas, blocks_here, capacity):
    owners_grid = owners_all.reshape(replicas, blocks_here)
    slots_grid = slots_all.reshape(replicas, blocks_here)
    ranks_grid = earlier_ranks(owners_grid)
    placed = (owners_grid == myself)[:, :, None] & (
        ranks_grid[:, :, None] == jnp.arange(capacity, dtype=jnp.int32)[None, None, :]
    )
    placed_int = placed.astype(jnp.int32)
    slot_index = jnp.sum(placed_int * slots_grid[:, :, None], axis=1).reshape(replicas * capacity)
    return (placed, slot_index)


def adapter_pass(slot_rows, slot_index, shrink_weights, pooled_up_weights, site_sum):
    chosen_shrink = jnp.take(shrink_weights, slot_index, axis=0)
    selected_expand = jnp.take(pooled_up_weights, slot_index, axis=0)
    partial_value = jnp.einsum(
        "snd,sdr->snr", slot_rows, chosen_shrink, preferred_element_type=jnp.float32
    )
    shrunk = site_sum(partial_value).astype(jnp.bfloat16)
    split_halves = shrunk.reshape(shrunk.shape[0], shrunk.shape[1], 2, shrunk.shape[2] // 2)
    summed_terms = jnp.einsum(
        "snkr,skrw->snkw", split_halves, selected_expand, preferred_element_type=jnp.float32
    )
    return (adapter_scale * summed_terms).astype(jnp.bfloat16)


def shards(
    hidden_in,
    queries,
    cache_keys,
    cached_value_rows,
    cache_lengths,
    base_key_matrix,
    base_value_matrix,
    shrink_weights,
    pooled_up_weights,
    block_owner,
    block_slot,
):
    rows_here = hidden_in.shape[0]
    shard_width = hidden_in.shape[1]
    replicas = lax.axis_size("rep")
    myself = lax.axis_index("rep")
    blocks_here = rows_here // BLK
    capacity = max(2, (2 * blocks_here + replicas - 1) // replicas)
    key_row_width = base_key_matrix.shape[1]
    gathered = lax.all_gather(hidden_in, "tp", axis=1, tiled=True)
    base_keys = jnp.dot(gathered, base_key_matrix, preferred_element_type=jnp.float32)
    base_values = jnp.dot(gathered, base_value_matrix, preferred_element_type=jnp.float32)
    owners_all, slots_all = (
        lax.all_gather(block_owner[:, 0], "rep", axis=0, tiled=True),
        lax.all_gather(block_slot, "rep", axis=0, tiled=True),
    )
    placed, slot_index = slot_layout(owners_all, slots_all, myself, replicas, blocks_here, capacity)
    every_row = lax.all_gather(hidden_in, "rep", axis=0, tiled=True)
    same_group = jnp.eye(replicas, dtype=jnp.bfloat16)
    compactor = jnp.einsum("pq,qbc->pcqb", same_group, placed.astype(jnp.bfloat16)).reshape(
        replicas * capacity, replicas * blocks_here
    )
    slot_rows = jnp.dot(
        compactor,
        every_row.reshape(replicas * blocks_here, BLK * shard_width),
        preferred_element_type=jnp.float32,
    ).astype(jnp.bfloat16)
    slot_rows = slot_rows.reshape(replicas * capacity, BLK, shard_width)

    def sum_every(partial_value):
        return lax.psum(partial_value, "tp")

    deltas = adapter_pass(slot_rows, slot_index, shrink_weights, pooled_up_weights, sum_every)
    spread = jnp.einsum(
        "sq,sx->qx",
        compactor,
        deltas.reshape(replicas * capacity, BLK * 2 * key_row_width),
        preferred_element_type=jnp.float32,
    )
    spread = spread.reshape(replicas * rows_here, 2, key_row_width)
    per_row_delta = lax.psum_scatter(
        spread.astype(jnp.bfloat16), "rep", scatter_dimension=0, tiled=True
    ).astype(jnp.float32)
    fresh_keys = (base_keys + per_row_delta[:, 0]).astype(jnp.bfloat16)
    fresh_values = (base_values + per_row_delta[:, 1]).astype(jnp.bfloat16)
    context = attend(
        queries, cache_keys, cached_value_rows, cache_lengths, fresh_keys, fresh_values
    )
    return (fresh_keys, fresh_values, context)


def solution(mesh):
    return jax.shard_map(
        shards,
        mesh=mesh,
        in_specs=(
            P("rep", "tp"),
            P("rep", "tp"),
            P("rep", None, "tp"),
            P("rep", None, "tp"),
            P("rep"),
            P(None, "tp"),
            P(None, "tp"),
            P("rep", "tp", None),
            P("rep", None, None, "tp"),
            P("rep", None),
            P("rep"),
        ),
        out_specs=(P("rep", "tp"), P("rep", "tp"), P("rep", "tp")),
        check_vma=False,
    )
```

profile of v0, /device:TPU:2, one launch (start us, length us, event | category | flops | bytes accessed | tf_op | source)
XLA Modules:
  0.0 236.1 jit_solution(2521708871560459143)
XLA Ops:
  8.0 0.0 all-gather.6.cloned.1.call-start
  8.1 0.7 all-gather.6.cloned.1.call-update
  8.8 0.0 reduce-scatter.2.cloned.1.call-start
  8.8 1.4 dynamic-slice
  10.9 0.9 dynamic-update-slice.1
  11.8 0.7 bitcast_dynamic-update-slice_fusion
  12.5 15.9 %all-reduce.2 = (s32[768]{0:T(1024)S(1)}, s32[768]{0:T(1024)S(1)}) all-reduce(s32[768]{0:T(1024)S(1)} %bitcast_dynamic-update-slice_fusion, s32[768]{0:T(1024)S(1)} %dynamic-update-slice.1), channel_id=2, replica_groups=mesh['rep'=32,'tp'=8] {'rep'}, use_global_device_ids=true, to_apply=%add | all-reduce | flops 1536 | bytes 12288
  28.4 0.1 reshape.169
  28.5 0.1 copy.23
  28.5 0.2 convert_reduce_fusion
  28.7 0.1 copy.25
  28.8 0.1 mul.45
  28.9 0.1 select_reduce_fusion.1
  29.0 0.1 copy.26
  29.1 0.1 reshape.172
  29.2 0.1 reshape.171
  29.3 1.0 multiply_bitcast_fusion
  30.3 1.7 reshape.170
  32.1 2.1 gather_fusion
  34.2 8.6 %gather_fusion.1 = bf16[64,1024,128]{2,1,0:T(8,128)(2,1)} fusion(bf16[4,1024,128]{2,1,0:T(8,128)(2,1)} %param.18, s32[1024]{0:T(1024)S(1)} %pad_clamp_fusion), kind=kCustom, calls=%fused_computation.1 | custom fusion | bytes 33554688 | tf_op jit(solution)/shard_map/jit(_take)/gather | solution.py:70
  42.8 24.6 %all-gather.6.cloned.1.call-done = bf16[3072,1024]{1,0:T(8,128)(2,1)} async-done(((bf16[96,1024]{1,0:T(8,128)(2,1)}), bf16[3072,1024]{1,0:T(8,128)(2,1)}) %all-gather.6.cloned.1.call-update) | async-done | bytes 6291472 | tf_op jit(solution)/shard_map/all_gather | solution.py:111
  67.4 10.7 %reshape.173 = bf16[768,4096]{1,0:T(8,128)(2,1)} reshape(bf16[3072,1024]{1,0:T(8,128)(2,1)} %all-gather.6.cloned.1.call-done) | data formatting | bytes 12582912 | tf_op jit(solution)/shard_map/reshape | solution.py:118
  78.1 4.8 %convolution_convert_fusion = bf16[64,4096]{1,0:T(8,128)(2,1)} fusion(bf16[64,768]{1,0:T(8,128)(2,1)S(1)} %reshape.170, bf16[768,4096]{1,0:T(8,128)(2,1)} %reshape.173), kind=kOutput, calls=%fused_computation.6 | convolution fusion | flops 402915328 | bytes 6914048 | tf_op jit(solution)/shard_map/dot_general | solution.py:116
  82.9 2.2 reshape.174
  85.1 8.7 %fusion = f32[64,4,128]{2,1,0:T(4,128)S(1)} fusion(bf16[64,4,1024]{2,1,0:T(4,128)(2,1)} %reshape.174, bf16[64,1024,128]{2,1,0:T(8,128)(2,1)} %gather_fusion.1, pred[64]{0:T(512)(128)(4,1)S(1)} %compare_and_fusion), kind=kOutput, calls=%fused_computation.2 | convolution fusion | flops 75497472 | bytes 17432640 | tf_op jit(solution)/shard_map/snd,sdr->snr/dot_general | solution.py:72
  93.7 31.5 %all-reduce.4 = bf16[64,4,128]{2,1,0:T(4,128)(2,1)S(1)} all-reduce(f32[64,4,128]{2,1,0:T(4,128)S(1)} %fusion), channel_id=1, replica_groups=mesh['rep'=32,'tp'=8] {'tp'}, use_global_device_ids=true, to_apply=%region_2.3 | all-reduce | flops 32768 | bytes 196608 | tf_op jit(solution)/shard_map/psum | solution.py:124
  125.2 0.1 reshape.175
  125.3 2.3 fusion.14
  127.6 0.1 copy.29
  127.8 0.1 reshape.176
  127.8 1.7 convolution_convert_fusion.1
  129.6 3.8 %convert_element_type.61 = bf16[3072,2,128]{2,1,0:T(2,128)(2,1)} reshape(bf16[768,1024]{1,0:T(8,128)(2,1)} %convolution_convert_fusion.1) | data formatting | bytes 3145728 | tf_op jit(solution)/shard_map/convert_element_type | solution.py:135
  133.4 2.8 %copy.30 = bf16[3072,2,128]{2,0,1:T(8,128)(2,1)} copy(bf16[3072,2,128]{2,1,0:T(2,128)(2,1)} %convert_element_type.61) | data formatting | bytes 3145728 | tf_op jit(solution)/shard_map/convert_element_type | solution.py:135
  136.2 0.0 reduce-scatter.2.cloned.1.call-update
  136.2 0.2 all-gather.4.cloned.1.call-start
  136.5 0.3 all-gather.4.cloned.1.call-update
  136.9 0.1 iota_compare_fusion
  137.0 0.6 copy-done.4
  137.5 2.4 %select_reduce_fusion = (f32[96,8]{1,0:T(8,128)}, f32[96,8,128]{2,1,0:T(8,128)S(1)}) fusion(pred[96,128]{1,0:T(8,128)(4,1)S(1)} %iota_compare_fusion, bf16[96,8,128]{2,1,0:T(8,128)(2,1)S(1)} %bitcast.43, bf16[96,128,128]{2,1,0:T(8,128)(2,1)S(1)} %copy-done), kind=kOutput, calls=%fused_computation.25 | convolution fusion | flops 25459968 | bytes 3750912 | tf_op jit(solution)/shard_map/rkgd,rtkd->rkgt/dot_general | solution.py:22
  140.0 79.3 %reduce-scatter.2.cloned.1.call-done = bf16[96,2,128]{2,0,1:T(8,128)(2,1)} async-done(((bf16[3072,2,128]{2,0,1:T(8,128)(2,1)}), bf16[96,2,128]{2,0,1:T(8,128)(2,1)}) %reduce-scatter.2.cloned.1.call-update) | async-done | bytes 49168 | tf_op jit(solution)/shard_map/reduce_scatter | solution.py:134
  219.3 1.4 convert_element_type.62
  220.8 2.8 %fusion.17 = bf16[96,128]{1,0:T(8,128)(2,1)S(1)} fusion(bf16[96,8192]{1,0:T(8,128)(2,1)} %all-gather.4.cloned.1.call-done, bf16[8192,128]{1,0:T(8,128)(2,1)} %param.16, f32[96,2,128]{2,0,1:T(8,128)} %convert_element_type.62), kind=kOutput, calls=%fused_computation.19 | convolution fusion | flops 201351168 | bytes 3743744 | tf_op jit(solution)/shard_map/dot_general | solution.py:104
  223.6 1.2 fusion.26
  224.8 0.3 fusion.20
  225.1 1.2 fusion.38
  226.3 0.6 copy-done.10
  227.0 1.0 fusion.7
  228.0 0.7 copy.40
  (33 shorter events, 0.2 us)
Async XLA Ops:
  8.0 129.6 %copy-start = (bf16[96,128,128]{2,1,0:T(8,128)(2,1)S(1)}, bf16[96,128,128]{2,1,0:T(8,128)(2,1)}, u32[]{:S(2)}) copy-start(bf16[96,128,128]{2,1,0:T(8,128)(2,1)} %param.13) | copy-start | bytes 9437188
  8.0 24.0 %copy-start.1 = (bf16[4,2,64,128]{3,2,1,0:T(8,128)(2,1)S(1)}, bf16[4,2,64,128]{3,2,1,0:T(8,128)(2,1)}, u32[]{:S(2)}) copy-start(bf16[4,2,64,128]{3,2,1,0:T(8,128)(2,1)} %param.19) | copy-start | bytes 393220
  8.0 59.3 %all-gather.6.cloned.1.call-start = ((), (), s32[]{:S(2)}) async-start(), calls=%async_computation.2 | async-start | bytes 6488064 | tf_op jit(solution)/shard_map/all_gather | solution.py:111
  8.8 210.6 %reduce-scatter.2.cloned.1.call-start = ((), (), s32[]{:S(2)}) async-start(), calls=%async_computation.3 | async-start | bytes 1622016 | tf_op jit(solution)/shard_map/reduce_scatter | solution.py:134
  133.4 3.4 %copy-start.7 = (bf16[96,1024]{1,0:T(8,128)(2,1)S(1)}, bf16[96,1024]{1,0:T(8,128)(2,1)}, u32[]{:S(2)}) copy-start(bf16[96,1024]{1,0:T(8,128)(2,1)} %param.12) | copy-start | bytes 589828
  133.4 3.5 %copy-start.9 = (s32[96]{0:T(128)S(1)}, s32[96]{0:T(128)}, u32[]{:S(2)}) copy-start(s32[96]{0:T(128)} %param.15) | copy-start | bytes 1156
  136.2 84.5 %all-gather.4.cloned.1.call-start = ((), (), s32[]{:S(2)}) async-start(), calls=%async_computation.1 | async-start | bytes 1769472 | tf_op jit(solution)/shard_map/all_gather | solution.py:103
  136.9 0.7 copy-start.4
  220.8 4.0 %copy-start.5 = (f32[96,8]{1,0:T(8,128)S(1)}, f32[96,8]{1,0:T(8,128)}, u32[]{:S(2)}) copy-start(f32[96,8]{1,0:T(8,128)} %get-tuple-element.9) | copy-start | bytes 9220
  220.8 4.4 %copy-start.2 = (bf16[96,8192]{1,0:T(8,128)(2,1)S(1)}, bf16[96,8192]{1,0:T(8,128)(2,1)}, u32[]{:S(2)}) copy-start(bf16[96,8192]{1,0:T(8,128)(2,1)} %all-gather.4.cloned.1.call-done) | copy-start | bytes 4718596
  220.8 4.4 %copy-start.3 = (bf16[8192,128]{1,0:T(8,128)(2,1)S(1)}, bf16[8192,128]{1,0:T(8,128)(2,1)}, u32[]{:S(2)}) copy-start(bf16[8192,128]{1,0:T(8,128)(2,1)} %param.17) | copy-start | bytes 6291460
  220.8 4.4 %copy-start.6 = (f32[96,2,128]{2,0,1:T(8,128)S(1)}, f32[96,2,128]{2,0,1:T(8,128)}, u32[]{:S(2)}) copy-start(f32[96,2,128]{2,0,1:T(8,128)} %convert_element_type.62) | copy-start | bytes 294916
  223.5 2.8 %copy-start.8 = (bf16[96,128]{1,0:T(8,128)(2,1)}, bf16[96,128]{1,0:T(8,128)(2,1)S(1)}, u32[]{:S(2)}) copy-start(bf16[96,128]{1,0:T(8,128)(2,1)S(1)} %fusion.17) | copy-start | bytes 73732
  225.1 1.9 copy-start.10
Sparse Core Ops, SparseCore 0:
  11.4 55.9 all-gather.5
  136.3 82.9 reduce-scatter.1
Sparse Core Ops, SparseCore 1:
  138.5 36.9 all-gather.3
where the time goes:
time: 237 us; the launch traced here: 236 us
  waiting for transfers between devices  105 us (44%)
  blocking collectives  47.3 us (20%)
  local copies, waits for them, and re-layouts  37.9 us (16%)
  matrix products  26 us (11%)
  between operations  16.4 us (7%)
  other arithmetic  3.18 us (1%)
    reduce_scatter x1, waiting for transfers between devices, shards(): lax.psum_scatter(spread.astype(jnp.bfloat16), 'rep', scatter_dimension=0,...  79.3 us
    psum x1, blocking collectives, sum_every(): return lax.psum(partial_value, 'tp')  31.5 us
    all_gather x1, waiting for transfers between devices, shards(): every_row = lax.all_gather(hidden_in, 'rep', axis=0, tiled=True)  24.6 us
    unnamed x1, blocking collectives  15.9 us
    reshape x1, local copies, waits for them, and re-layouts, shards(): every_row.reshape(replicas * blocks_here, BLK * shard_width)  10.7 us
    dot_general x1, matrix products, adapter_pass(): jnp.einsum('snd,sdr->snr', slot_rows, chosen_shrink, preferred_element_ty...  8.66 us
    gather x1, local copies, waits for them, and re-layouts, adapter_pass(): chosen_shrink = jnp.take(shrink_weights, slot_index, axis=0)  8.6 us
    convert_element_type x2, local copies, waits for them, and re-layouts, shards(): spread.astype(jnp.bfloat16)  6.61 us
  transfers between devices with their start and end apart: 3, of which 2 were waited for; matrix products, arithmetic and copies ran while one was open for 9% of the time, Pallas kernels for 0%

commit v1 on v0

--- a/solution.py
+++ b/solution.py
@@ -108,7 +108,9 @@
         lax.all_gather(block_slot, "rep", axis=0, tiled=True),
     )
     placed, slot_index = slot_layout(owners_all, slots_all, myself, replicas, blocks_here, capacity)
-    every_row = lax.all_gather(hidden_in, "rep", axis=0, tiled=True)
+    every_row = jnp.concatenate(
+        lax.all_to_all(jnp.stack([hidden_in] * lax.axis_size("rep")), "rep", 0, 0), axis=0
+    )
     same_group = jnp.eye(replicas, dtype=jnp.bfloat16)
     compactor = jnp.einsum("pq,qbc->pcqb", same_group, placed.astype(jnp.bfloat16)).reshape(
         replicas * capacity, replicas * blocks_here

time: 237 us -> 295 us (1.24)
  blocking collectives: 47.3 us -> 114 us
  waiting for transfers between devices: 105 us -> 86 us
  starting transfers between devices: 0.3 us -> 8.07 us
    unnamed x1, blocking collectives: 15.9 us -> 79.9 us
    all_gather x1 -> x0, waiting for transfers between devices: 24.6 us -> none  [shards(): every_row = lax.all_gather(hidden_in, 'rep', axis=0, tiled=True)]
    another operation x0 -> x2, local copies, waits for them, and re-layouts: none -> 15.3 us  [the longest x1 10.7 us: shards(): every_row.reshape(replicas * blocks_here, BLK * shard_width)]
    reshape x1 -> x0, local copies, waits for them, and re-layouts: 10.7 us -> none  [shards(): every_row.reshape(replicas * blocks_here, BLK * shard_width)]
    all_to_all x0 -> x1, starting transfers between devices: none -> 7.81 us  [shards(): lax.all_to_all(jnp.stack([hidden_in] * lax.axis_size('rep')), 'rep', 0, 0)]
    reduce_scatter x1, waiting for transfers between devices: 79.3 us -> 85.6 us  [shards(): lax.psum_scatter(spread.astype(jnp.bfloat16), 'rep', scatter_dimension=0,...]
  transfers between devices with their start and end apart: 3 -> 3, of which waited for: 2 -> 1; matrix products, arithmetic and copies ran while one was open for 9% -> 7% of each run, Pallas kernels for 0% -> 0%
where the time goes in v1:
time: 295 us; the launch traced here: 294 us
  blocking collectives  114 us (39%)
  waiting for transfers between devices  86 us (29%)
  local copies, waits for them, and re-layouts  40.3 us (14%)
  matrix products  26.1 us (9%)
  between operations  16.4 us (6%)
  starting transfers between devices  8.07 us (3%)
  other arithmetic  3.17 us (1%)
    reduce_scatter x1, waiting for transfers between devices, shards(): lax.psum_scatter(spread.astype(jnp.bfloat16), 'rep', scatter_dimension=0,...  85.6 us
    unnamed x1, blocking collectives  79.9 us
    psum x1, blocking collectives, sum_every(): return lax.psum(partial_value, 'tp')  34 us
    another operation x1, local copies, waits for them, and re-layouts, shards(): every_row.reshape(replicas * blocks_here, BLK * shard_width)  10.7 us
    dot_general x1, matrix products, adapter_pass(): jnp.einsum('snd,sdr->snr', slot_rows, chosen_shrink, preferred_element_ty...  8.66 us
    gather x1, local copies, waits for them, and re-layouts, adapter_pass(): chosen_shrink = jnp.take(shrink_weights, slot_index, axis=0)  8.59 us
    all_to_all x1, starting transfers between devices, shards(): lax.all_to_all(jnp.stack([hidden_in] * lax.axis_size('rep')), 'rep', 0, 0)  7.81 us
    convert_element_type x2, local copies, waits for them, and re-layouts, shards(): spread.astype(jnp.bfloat16)  6.6 us
  transfers between devices with their start and end apart: 3, of which 1 were waited for; matrix products, arithmetic and copies ran while one was open for 7% of the time, Pallas kernels for 0%

profile of v1, /device:TPU:2, one launch (start us, length us, event | category | flops | bytes accessed | tf_op | source)
XLA Modules:
  0.0 294.0 jit_solution(8083053023596823827)
XLA Ops:
  8.0 0.0 copy-start
  8.0 4.5 %stack.2 = bf16[32,96,1024]{2,1,0:T(8,128)(2,1)} broadcast(bf16[96,1024]{1,0:T(8,128)(2,1)} %param.11), dimensions={1,2} | broadcast | bytes 6488064 | tf_op jit(solution)/shard_map/stack | solution.py:112
  12.5 7.8 %all-to-all-start = ((bf16[32,96,1024]{2,1,0:T(8,128)(2,1)}), bf16[32,96,1024]{2,1,0:T(8,128)(2,1)}, u32[]{:S(2)}, u32[]{:S(2)}) async-start(bf16[32,96,1024]{2,1,0:T(8,128)(2,1)} %stack.2), calls=%async_computation | async-start | bytes 12582912 | tf_op jit(solution)/shard_map/all_to_all | solution.py:112
  20.4 0.0 reduce-scatter.2.cloned.1.call-start
  20.4 0.6 dynamic-slice
  21.7 0.2 dynamic-update-slice.1
  21.9 0.1 bitcast_dynamic-update-slice_fusion
  22.0 79.9 %all-reduce.2 = (s32[768]{0:T(1024)S(1)}, s32[768]{0:T(1024)S(1)}) all-reduce(s32[768]{0:T(1024)S(1)} %bitcast_dynamic-update-slice_fusion, s32[768]{0:T(1024)S(1)} %dynamic-update-slice.1), channel_id=2, replica_groups=mesh['rep'=32,'tp'=8] {'rep'}, use_global_device_ids=true, to_apply=%add | all-reduce | flops 1536 | bytes 12288
  101.9 0.1 reshape.168
  102.0 0.1 copy.23
  102.1 0.2 convert_reduce_fusion
  102.3 0.1 copy.25
  102.3 0.1 mul.45
  102.5 0.1 select_reduce_fusion.1
  102.6 0.1 copy.26
  102.7 0.1 reshape.171
  102.8 0.1 reshape.170
  102.9 1.0 multiply_bitcast_fusion
  103.9 1.7 reshape.169
  105.6 2.2 gather_fusion
  107.8 8.6 %gather_fusion.1 = bf16[64,1024,128]{2,1,0:T(8,128)(2,1)} fusion(bf16[4,1024,128]{2,1,0:T(8,128)(2,1)} %param.18, s32[1024]{0:T(1024)S(1)} %pad_clamp_fusion), kind=kCustom, calls=%fused_computation.1 | custom fusion | bytes 33554688 | tf_op jit(solution)/shard_map/jit(_take)/gather | solution.py:70
  116.4 10.7 %reshape_reshape.3 = bf16[768,4096]{1,0:T(8,128)(2,1)} reshape(bf16[32,96,1024]{2,1,0:T(8,128)(2,1)} %all-to-all-done) | data formatting | bytes 12582912 | tf_op jit(solution)/shard_map/reshape;reshape | solution.py:120
  127.1 4.8 %convolution_convert_fusion = bf16[64,4096]{1,0:T(8,128)(2,1)} fusion(bf16[64,768]{1,0:T(8,128)(2,1)S(1)} %reshape.169, bf16[768,4096]{1,0:T(8,128)(2,1)} %reshape_reshape.3), kind=kOutput, calls=%fused_computation.6 | convolution fusion | flops 402915328 | bytes 6914048 | tf_op jit(solution)/shard_map/dot_general | solution.py:118
  131.9 2.2 reshape.172
  134.1 8.7 %fusion = f32[64,4,128]{2,1,0:T(4,128)S(1)} fusion(bf16[64,4,1024]{2,1,0:T(4,128)(2,1)} %reshape.172, bf16[64,1024,128]{2,1,0:T(8,128)(2,1)} %gather_fusion.1, pred[64]{0:T(512)(128)(4,1)S(1)} %compare_and_fusion), kind=kOutput, calls=%fused_computation.2 | convolution fusion | flops 75497472 | bytes 17432640 | tf_op jit(solution)/shard_map/snd,sdr->snr/dot_general | solution.py:72
  142.8 34.0 %all-reduce.4 = bf16[64,4,128]{2,1,0:T(4,128)(2,1)S(1)} all-reduce(f32[64,4,128]{2,1,0:T(4,128)S(1)} %fusion), channel_id=1, replica_groups=mesh['rep'=32,'tp'=8] {'tp'}, use_global_device_ids=true, to_apply=%region_2.3 | all-reduce | flops 32768 | bytes 196608 | tf_op jit(solution)/shard_map/psum | solution.py:126
  176.8 0.1 reshape.173
  176.9 2.3 fusion.14
  179.2 0.1 copy.29
  179.3 0.1 reshape.174
  179.4 1.7 convolution_convert_fusion.1
  181.2 3.8 %convert_element_type.61 = bf16[3072,2,128]{2,1,0:T(2,128)(2,1)} reshape(bf16[768,1024]{1,0:T(8,128)(2,1)} %convolution_convert_fusion.1) | data formatting | bytes 3145728 | tf_op jit(solution)/shard_map/convert_element_type | solution.py:137
  185.0 2.8 copy.30
  187.8 0.0 reduce-scatter.2.cloned.1.call-update
  187.8 0.2 all-gather.3.cloned.1.call-start
  188.0 0.3 all-gather.3.cloned.1.call-update
  188.4 0.1 iota_compare_fusion
  188.5 0.6 copy-done.4
  189.1 2.4 select_reduce_fusion
  191.5 85.6 %reduce-scatter.2.cloned.1.call-done = bf16[96,2,128]{2,0,1:T(8,128)(2,1)} async-done(((bf16[3072,2,128]{2,0,1:T(8,128)(2,1)}), bf16[96,2,128]{2,0,1:T(8,128)(2,1)}) %reduce-scatter.2.cloned.1.call-update) | async-done | bytes 49168 | tf_op jit(solution)/shard_map/reduce_scatter | solution.py:136
  277.2 1.4 convert_element_type.62
  278.6 2.8 fusion.17
  281.4 1.2 fusion.26
  282.6 0.3 fusion.20
  283.0 1.2 fusion.38
  284.2 0.6 copy-done.10
  284.8 1.0 fusion.7
  285.8 0.7 copy.40
  (39 shorter events, 0.2 us)
Async XLA Ops:
  8.0 181.1 %copy-start = (bf16[96,128,128]{2,1,0:T(8,128)(2,1)S(1)}, bf16[96,128,128]{2,1,0:T(8,128)(2,1)}, u32[]{:S(2)}) copy-start(bf16[96,128,128]{2,1,0:T(8,128)(2,1)} %param.13) | copy-start | bytes 9437188
  12.5 7.9 %copy-start.13 = (u32[256]{0:T(256)S(1)}, u32[256]{0:T(256)}, u32[]{:S(2)}) copy-start(u32[256]{0:T(256)} %constant.53) | copy-start | bytes 3076
  12.5 9.1 %copy-start.11 = (s32[24]{0:T(128)S(1)}, s32[24]{0:T(128)}, u32[]{:S(2)}) copy-start(s32[24]{0:T(128)} %param.21) | copy-start | bytes 292
  12.5 9.4 %copy-start.12 = (s32[24,1]{0,1:T(1,128)S(1)}, s32[24,1]{0,1:T(1,128)}, u32[]{:S(2)}) copy-start(s32[24,1]{0,1:T(1,128)} %param.20) | copy-start | bytes 292
  12.5 103.8 %all-to-all-start = ((bf16[32,96,1024]{2,1,0:T(8,128)(2,1)}), bf16[32,96,1024]{2,1,0:T(8,128)(2,1)}, u32[]{:S(2)}, u32[]{:S(2)}) async-start(bf16[32,96,1024]{2,1,0:T(8,128)(2,1)} %stack.2), calls=%async_computation | async-start | bytes 12582912 | tf_op jit(solution)/shard_map/all_to_all | solution.py:112
  20.4 85.3 %copy-start.1 = (bf16[4,2,64,128]{3,2,1,0:T(8,128)(2,1)S(1)}, bf16[4,2,64,128]{3,2,1,0:T(8,128)(2,1)}, u32[]{:S(2)}) copy-start(bf16[4,2,64,128]{3,2,1,0:T(8,128)(2,1)} %param.19) | copy-start | bytes 393220
  20.4 256.8 %reduce-scatter.2.cloned.1.call-start = ((), (), s32[]{:S(2)}) async-start(), calls=%async_computation.3 | async-start | bytes 1622016 | tf_op jit(solution)/shard_map/reduce_scatter | solution.py:136
  185.0 3.4 %copy-start.7 = (bf16[96,1024]{1,0:T(8,128)(2,1)S(1)}, bf16[96,1024]{1,0:T(8,128)(2,1)}, u32[]{:S(2)}) copy-start(bf16[96,1024]{1,0:T(8,128)(2,1)} %param.12) | copy-start | bytes 589828
  185.0 3.5 %copy-start.9 = (s32[96]{0:T(128)S(1)}, s32[96]{0:T(128)}, u32[]{:S(2)}) copy-start(s32[96]{0:T(128)} %param.15) | copy-start | bytes 1156
  187.8 90.8 %all-gather.3.cloned.1.call-start = ((), (), s32[]{:S(2)}) async-start(), calls=%async_computation.2 | async-start | bytes 1769472 | tf_op jit(solution)/shard_map/all_gather | solution.py:103
  188.4 0.7 copy-start.4
  278.6 4.0 %copy-start.5 = (f32[96,8]{1,0:T(8,128)S(1)}, f32[96,8]{1,0:T(8,128)}, u32[]{:S(2)}) copy-start(f32[96,8]{1,0:T(8,128)} %get-tuple-element.9) | copy-start | bytes 9220
  278.6 4.4 %copy-start.2 = (bf16[96,8192]{1,0:T(8,128)(2,1)S(1)}, bf16[96,8192]{1,0:T(8,128)(2,1)}, u32[]{:S(2)}) copy-start(bf16[96,8192]{1,0:T(8,128)(2,1)} %all-gather.3.cloned.1.call-done) | copy-start | bytes 4718596
  278.6 4.4 %copy-start.3 = (bf16[8192,128]{1,0:T(8,128)(2,1)S(1)}, bf16[8192,128]{1,0:T(8,128)(2,1)}, u32[]{:S(2)}) copy-start(bf16[8192,128]{1,0:T(8,128)(2,1)} %param.17) | copy-start | bytes 6291460
  278.6 4.4 %copy-start.6 = (f32[96,2,128]{2,0,1:T(8,128)S(1)}, f32[96,2,128]{2,0,1:T(8,128)}, u32[]{:S(2)}) copy-start(f32[96,2,128]{2,0,1:T(8,128)} %convert_element_type.62) | copy-start | bytes 294916
  281.4 2.8 copy-start.8
  282.9 1.9 copy-start.10
Sparse Core Ops, SparseCore 0:
  187.9 89.2 reduce-scatter.1
Sparse Core Ops, SparseCore 1:
  190.1 43.2 all-gather.2
